TPU v7x, 32 devices: a whole 2x2x4 slice. The times are simulated.
32 devices in a mesh: seg: 8 (over z, core), seq: 4 (over y, x).
Axes of the slice: x: 2, y: 2, z: 4, core: 2. Of those that a mesh axis runs over, the one named last changes fastest.
Arguments:
- layer_input: bfloat16 [8, 2048, 1024], P('seg', 'seq'), may hold values from -6 to 6
- output_grad: bfloat16 [8, 2048, 1024], P('seg', 'seq'), may hold values from -6 to 6
- norm1_gain: float32 [1024], replicated, may hold values from 0.5 to 1.5
- norm2_gain: float32 [1024], replicated, may hold values from 0.5 to 1.5
- w_qkv: bfloat16 [1024, 3072], replicated, may hold values from -0.25 to 0.25
- w_out: bfloat16 [1024, 1024], replicated, may hold values from -0.75 to 0.75
- w_gate: bfloat16 [1024, 2816], replicated, may hold values from -0.1875 to 0.1875
- w_up: bfloat16 [1024, 2816], replicated, may hold values from -0.1875 to 0.1875
- w_down: bfloat16 [2816, 1024], replicated, may hold values from -0.109375 to 0.109375
- mem_keys: bfloat16 [8, 1024, 1024], P('seg', 'seq'), may hold values from -8 to 8
- mem_values: bfloat16 [8, 1024, 1024], P('seg', 'seq'), may hold values from -8 to 8
- memory_flags: int32 [8], replicated, may hold values from 0 to 1, as said below
- sources: int32 [8, 3], replicated, may hold values from 0 to 7, as said below
Outputs:
- output: bfloat16 [8, 2048, 1024], P('seg', 'seq')
- input_grad: float32 [8, 2048, 1024], P('seg', 'seq')
- grad_norm1: float32 [1024], P('seq')
- grad_norm2: float32 [1024], P('seq')
- grad_qkv: float32 [1024, 3072], P('seq')
- grad_out: float32 [1024, 1024], P('seq')
- grad_gate: float32 [1024, 2816], P('seq')
- grad_up: float32 [1024, 2816], P('seq')
- grad_down: float32 [2816, 1024], P('seq')
Inputs may be any that keep to these rules, and one draw needn't show every extreme that they name: `memory_flags`: exactly half of the segments have flag 1. `sources`: row s lists 3 different segments, none of them s. The first column is a permutation of the segments, and the first source of a segment has the other flag than the segment.
All inputs are finite; a program needn't handle non-finite values.
Results may differ from a plain program's by a relative error of at most 0.023.
Values may be sent and summed in bfloat16 or wider, within the bound.
A program may use at most 256 MiB of HBM per device.

v0:
```python
import jax
import jax.numpy as jnp
from jax import lax
from jax.sharding import PartitionSpec as P

D = 1024
HEADS = 8
HEAD_DIM = 128
masked_score = -1e30
epsilon = 1e-06
rotary_base = 10000.0


def product(former, latter):
    return jnp.dot(former, latter, preferred_element_type=jnp.float32)


def product_nt(former, latter):
    return lax.dot_general(
        former, latter, (((1,), (1,)), ((), ())), preferred_element_type=jnp.float32
    )


def product_tn(former, latter):
    return lax.dot_general(
        former, latter, (((0,), (0,)), ((), ())), preferred_element_type=jnp.float32
    )


def norm_forward(values, norm_gain):
    inverse = lax.rsqrt(jnp.mean(values * values, axis=-1, keepdims=True) + epsilon)
    return (values * inverse * norm_gain, inverse)


def norm_backward(values, inverse, norm_gain, upstream):
    weighted = upstream * norm_gain
    inner_mean = jnp.mean(weighted * values, axis=-1, keepdims=True)
    grad_values = inverse * weighted - inverse * inverse * inverse * values * inner_mean
    grad_gain = jnp.sum(upstream * values * inverse, axis=0)
    return (grad_values, grad_gain)


def turn_tables(positions):
    half_dim = HEAD_DIM // 2
    exponent = -2.0 * jnp.arange(half_dim, dtype=jnp.float32) / HEAD_DIM
    angles = positions[:, None] * jnp.power(rotary_base, exponent)[None, :]
    angles = jnp.concatenate([angles, angles], axis=1)
    return (jnp.cos(angles)[:, None, :], jnp.sin(angles)[:, None, :])


def rotate(matrix, cosine_table, sine_table, direction):
    row_count = matrix.shape[0]
    half_dim = HEAD_DIM // 2
    shaped = matrix.reshape(row_count, HEADS, HEAD_DIM)
    turned = jnp.concatenate([-shaped[..., half_dim:], shaped[..., :half_dim]], axis=-1)
    return (shaped * cosine_table + direction * turned * sine_table).reshape(
        row_count, HEADS * HEAD_DIM
    )


def on_device(
    layer_input,
    output_grad,
    norm1_gain,
    norm2_gain,
    w_qkv,
    w_out,
    w_gate,
    w_up,
    w_down,
    mem_keys,
    mem_values,
    memory_flags,
    sources,
):
    seg_index = lax.axis_index("seg")
    seq_index = lax.axis_index("seq")
    tokens = layer_input.shape[1]
    score_scale = HEAD_DIM ** (-0.5)
    flag_on = lax.dynamic_index_in_dim(memory_flags, seg_index, 0, keepdims=False) > 0
    listed = lax.dynamic_index_in_dim(sources, seg_index, 0, keepdims=False)
    picked = jnp.concatenate([jnp.reshape(seg_index, (1,)), listed])
    every_keys, every_values = (
        lax.all_gather(mem_keys, "seg", axis=0, tiled=True),
        lax.all_gather(mem_values, "seg", axis=0, tiled=True),
    )
    chosen_keys = jnp.take(every_keys, picked, axis=0)
    chosen_values = jnp.take(every_values, picked, axis=0)
    memory_keys, memory_values = (
        lax.all_gather(chosen_keys, "seq", axis=1, tiled=True),
        lax.all_gather(chosen_values, "seq", axis=1, tiled=True),
    )
    memory_key_blocks = memory_keys.reshape(-1, tokens, HEADS, HEAD_DIM)
    memory_value_blocks = memory_values.reshape(-1, tokens, HEADS, HEAD_DIM)
    memory_blocks = memory_key_blocks.shape[0]
    inputs = layer_input[0].astype(jnp.float32)
    first_norm, first_inverse = norm_forward(inputs, norm1_gain)
    first_low = first_norm.astype(jnp.bfloat16)
    projected = product(first_low, w_qkv)
    positions = seq_index * tokens + lax.iota(jnp.int32, tokens)
    cosine_table, sine_table = turn_tables(positions.astype(jnp.float32))
    queries = rotate(projected[:, :D], cosine_table, sine_table, 1.0).astype(jnp.bfloat16)
    own_keys = rotate(projected[:, D : 2 * D], cosine_table, sine_table, 1.0).astype(jnp.bfloat16)
    own_values = projected[:, 2 * D :].astype(jnp.bfloat16)
    all_keys, all_values = (
        lax.all_gather(own_keys, "seq", axis=0, tiled=True),
        lax.all_gather(own_values, "seq", axis=0, tiled=True),
    )
    key_blocks = all_keys.reshape(-1, tokens, HEADS, HEAD_DIM)
    value_blocks = all_values.reshape(-1, tokens, HEADS, HEAD_DIM)
    query_heads = queries.reshape(tokens, HEADS, HEAD_DIM)
    memory_open = jnp.broadcast_to(flag_on, (tokens, tokens))
    own_count = seq_index + 1
    key_offsets = lax.iota(jnp.int32, tokens)

    def own_open(block):
        return (block * tokens + key_offsets)[None, :] <= positions[:, None]

    def block_scores(key_block, open_mask):
        raw = (
            jnp.einsum("qhd,khd->hqk", query_heads, key_block, preferred_element_type=jnp.float32)
            * score_scale
        )
        return jnp.where(open_mask[None], raw, masked_score)

    def sweep(step, carry):

        def memory_turn(block, state):
            return step(
                state,
                block,
                memory_key_blocks[block],
                memory_value_blocks[block],
                memory_open,
                False,
            )

        def own_turn(block, state):
            return step(state, block, key_blocks[block], value_blocks[block], own_open(block), True)

        carry = lax.fori_loop(0, memory_blocks, memory_turn, carry)
        return lax.fori_loop(0, own_count, own_turn, carry)

    def max_step(carry, block, key_block, value_block, open_mask, own):
        row_max, row_sum = carry
        scores = block_scores(key_block, open_mask)
        new_max = jnp.maximum(row_max, jnp.max(scores, axis=2))
        row_sum = row_sum * jnp.exp(row_max - new_max) + jnp.sum(
            jnp.exp(scores - new_max[..., None]), axis=2
        )
        return (new_max, row_sum)

    start_max = jnp.full((HEADS, tokens), masked_score, jnp.float32)
    row_max, row_sum = sweep(max_step, (start_max, jnp.zeros((HEADS, tokens), jnp.float32)))
    log_totals = row_max + jnp.log(row_sum)

    def mix_step(total, block, key_block, value_block, open_mask, own):
        weights_low = jnp.exp(block_scores(key_block, open_mask) - log_totals[..., None]).astype(
            jnp.bfloat16
        )
        return total + jnp.einsum(
            "hqk,khd->qhd", weights_low, value_block, preferred_element_type=jnp.float32
        )

    attended = sweep(mix_step, jnp.zeros((tokens, HEADS, HEAD_DIM), jnp.float32))
    attended_low = attended.reshape(tokens, D).astype(jnp.bfloat16)
    residual = inputs + product(attended_low, w_out)
    second_norm, second_inverse = norm_forward(residual, norm2_gain)
    second_low = second_norm.astype(jnp.bfloat16)
    gate_values = product(second_low, w_gate)
    up_values = product(second_low, w_up)
    sigmoid_gate = jax.nn.sigmoid(gate_values)
    activated = gate_values * sigmoid_gate
    hidden_low = (activated * up_values).astype(jnp.bfloat16)
    output = (residual + product(hidden_low, w_down)).astype(jnp.bfloat16)
    upstream = output_grad[0]
    grad_down = product_tn(hidden_low, upstream)
    grad_hidden = product_nt(upstream, w_down)
    grad_gate_low = (
        grad_hidden * up_values * sigmoid_gate * (1.0 + gate_values * (1.0 - sigmoid_gate))
    ).astype(jnp.bfloat16)
    grad_up_low = (grad_hidden * activated).astype(jnp.bfloat16)
    grad_gate = product_tn(second_low, grad_gate_low)
    grad_up = product_tn(second_low, grad_up_low)
    grad_second = product_nt(grad_gate_low, w_gate) + product_nt(grad_up_low, w_up)
    grad_residual, grad_norm2 = norm_backward(residual, second_inverse, norm2_gain, grad_second)
    grad_residual = grad_residual + upstream.astype(jnp.float32)
    residual_low = grad_residual.astype(jnp.bfloat16)
    grad_out = product_tn(attended_low, residual_low)
    grad_attended = product_nt(residual_low, w_out).astype(jnp.bfloat16)
    grad_heads = grad_attended.reshape(tokens, HEADS, HEAD_DIM)

    def probs_pair(key_block, value_block, open_mask):
        probs = jnp.exp(block_scores(key_block, open_mask) - log_totals[..., None])
        dprobs = jnp.einsum(
            "qhd,khd->hqk", grad_heads, value_block, preferred_element_type=jnp.float32
        )
        return (probs, dprobs)

    def delta_step(total, block, key_block, value_block, open_mask, own):
        probs, dprobs = probs_pair(key_block, value_block, open_mask)
        return total + jnp.sum(probs * dprobs, axis=2)

    delta_rows = sweep(delta_step, jnp.zeros((HEADS, tokens), jnp.float32))

    def grad_step(carry, block, key_block, value_block, open_mask, own):
        grad_query, key_terms, value_terms = carry
        probs, dprobs = probs_pair(key_block, value_block, open_mask)
        dscores = (probs * (dprobs - delta_rows[..., None])).astype(jnp.bfloat16)
        grad_query = grad_query + jnp.einsum(
            "hqk,khd->qhd", dscores, key_block, preferred_element_type=jnp.float32
        )
        if own:
            key_part = (
                jnp.einsum("hqk,qhd->khd", dscores, query_heads, preferred_element_type=jnp.float32)
                * score_scale
            )
            value_part = jnp.einsum(
                "hqk,qhd->khd",
                probs.astype(jnp.bfloat16),
                grad_heads,
                preferred_element_type=jnp.float32,
            )
            key_terms = lax.dynamic_update_index_in_dim(key_terms, key_part, block, 0)
            value_terms = lax.dynamic_update_index_in_dim(value_terms, value_part, block, 0)
        return (grad_query, key_terms, value_terms)

    term_shape = key_blocks.shape
    start_grads = (
        jnp.zeros((tokens, HEADS, HEAD_DIM), jnp.float32),
        jnp.zeros(term_shape, jnp.float32),
        jnp.zeros(term_shape, jnp.float32),
    )
    grad_query, key_terms, value_terms = sweep(grad_step, start_grads)
    grad_queries = (grad_query * score_scale).reshape(tokens, D)
    grad_keys, grad_values = (
        lax.psum_scatter(
            key_terms.astype(jnp.bfloat16), "seq", scatter_dimension=0, tiled=True
        ).astype(jnp.float32),
        lax.psum_scatter(
            value_terms.astype(jnp.bfloat16), "seq", scatter_dimension=0, tiled=True
        ).astype(jnp.float32),
    )
    grad_projected = jnp.concatenate(
        [
            rotate(grad_queries, cosine_table, sine_table, -1.0),
            rotate(grad_keys.reshape(tokens, D), cosine_table, sine_table, -1.0),
            grad_values.reshape(tokens, D),
        ],
        axis=1,
    ).astype(jnp.bfloat16)
    grad_qkv = product_tn(first_low, grad_projected)
    grad_first = product_nt(grad_projected, w_qkv)
    grad_inputs, grad_norm1 = norm_backward(inputs, first_inverse, norm1_gain, grad_first)
    input_grad = (grad_inputs + grad_residual)[None]
    shares = (
        lax.psum_scatter(
            grad_norm1.astype(jnp.bfloat16), "seq", scatter_dimension=0, tiled=True
        ).astype(jnp.float32),
        lax.psum_scatter(
            grad_norm2.astype(jnp.bfloat16), "seq", scatter_dimension=0, tiled=True
        ).astype(jnp.float32),
        lax.psum_scatter(
            grad_qkv.astype(jnp.bfloat16), "seq", scatter_dimension=0, tiled=True
        ).astype(jnp.float32),
        lax.psum_scatter(
            grad_out.astype(jnp.bfloat16), "seq", scatter_dimension=0, tiled=True
        ).astype(jnp.float32),
        lax.psum_scatter(
            grad_gate.astype(jnp.bfloat16), "seq", scatter_dimension=0, tiled=True
        ).astype(jnp.float32),
        lax.psum_scatter(
            grad_up.astype(jnp.bfloat16), "seq", scatter_dimension=0, tiled=True
        ).astype(jnp.float32),
        lax.psum_scatter(
            grad_down.astype(jnp.bfloat16), "seq", scatter_dimension=0, tiled=True
        ).astype(jnp.float32),
    )
    totals = (
        lax.psum(shares[0].astype(jnp.bfloat16), "seg").astype(jnp.float32),
        lax.psum(shares[1].astype(jnp.bfloat16), "seg").astype(jnp.float32),
        lax.psum(shares[2].astype(jnp.bfloat16), "seg").astype(jnp.float32),
        lax.psum(shares[3].astype(jnp.bfloat16), "seg").astype(jnp.float32),
        lax.psum(shares[4].astype(jnp.bfloat16), "seg").astype(jnp.float32),
        lax.psum(shares[5].astype(jnp.bfloat16), "seg").astype(jnp.float32),
        lax.psum(shares[6].astype(jnp.bfloat16), "seg").astype(jnp.float32),
    )
    return (
        output[None],
        input_grad,
        totals[0],
        totals[1],
        totals[2],
        totals[3],
        totals[4],
        totals[5],
        totals[6],
    )


def solution(mesh):
    placed = (
        P("seg", "seq", None),
        P("seg", "seq", None),
        P(),
        P(),
        P(),
        P(),
        P(),
        P(),
        P(),
        P("seg", "seq", None),
        P("seg", "seq", None),
        P(),
        P(),
    )
    return jax.shard_map(
        on_device,
        mesh=mesh,
        in_specs=placed,
        out_specs=(
            P("seg", "seq", None),
            P("seg", "seq", None),
            P("seq"),
            P("seq"),
            P("seq", None),
            P("seq", None),
            P("seq", None),
            P("seq", None),
            P("seq", None),
        ),
        check_vma=False,
    )
```

profile of v0, /device:TPU:0, one launch (start us, length us, event | category | flops | bytes accessed | tf_op | source)
XLA Modules:
  0.0 1502.4 jit_solution(4767216906355732668)
XLA Ops:
  39.9 19.3 %all-gather.7.cloned.1.call-done = bf16[8,256,1024]{2,1,0:T(8,128)(2,1)} async-done(((bf16[1,256,1024]{2,1,0:T(8,128)(2,1)}), bf16[8,256,1024]{2,1,0:T(8,128)(2,1)}) %all-gather.7.cloned.1.call-update) | async-done | bytes 4194320 | tf_op jit(solution)/shard_map/all_gather | solution.py:85
  63.4 43.1 %all-gather.11.cloned.1.call-done = bf16[8,256,1024]{2,1,0:T(8,128)(2,1)} async-done(((bf16[1,256,1024]{2,1,0:T(8,128)(2,1)}), bf16[8,256,1024]{2,1,0:T(8,128)(2,1)}) %all-gather.11.cloned.1.call-update) | async-done | bytes 4194320 | tf_op jit(solution)/shard_map/all_gather | solution.py:84
  118.4 41.9 %all-gather.15.cloned.1.call-done = bf16[2048,1024]{1,0:T(8,128)(2,1)} async-done(((bf16[512,1024]{1,0:T(8,128)(2,1)}), bf16[2048,1024]{1,0:T(8,128)(2,1)}) %all-gather.15.cloned.1.call-update) | async-done | bytes 4194320 | tf_op jit(solution)/shard_map/all_gather | solution.py:106
  166.5 48.7 %all-gather.17.cloned.1.call-done = bf16[2048,1024]{1,0:T(8,128)(2,1)} async-done(((bf16[512,1024]{1,0:T(8,128)(2,1)}), bf16[2048,1024]{1,0:T(8,128)(2,1)}) %all-gather.17.cloned.1.call-update) | async-done | bytes 4194320 | tf_op jit(solution)/shard_map/all_gather | solution.py:107
  221.9 83.1 %all-gather.13.cloned.1.call-done = bf16[4,1024,1024]{2,1,0:T(8,128)(2,1)} async-done(((bf16[4,256,1024]{2,1,0:T(8,128)(2,1)}), bf16[4,1024,1024]{2,1,0:T(8,128)(2,1)}) %all-gather.13.cloned.1.call-update) | async-done | bytes 8388624 | tf_op jit(solution)/shard_map/all_gather | solution.py:90
  305.0 8.9 copy.127
  313.9 10.1 copy.87
  324.0 88.0 %while.112 = (s32[]{:T(128)}, f32[8,512]{1,0:T(8,128)S(1)}, f32[8,512]{1,0:T(8,128)S(1)}, bf16[8,512,8,128]{3,1,2,0:T(8,128)(2,1)}, bf16[512,8,128]{2,0,1:T(8,128)(2,1)S(1)}, /*index=5*/pred[]{:T(512)}, s32[]{:T(128)}, s32[]{:T(128)}) while((s32[]{:T(128)}, f32[8,512]{1,0:T(8,128)S(1)}, f32[8,512]{1,0:T(8,128)S(1)}, ...), condition=%wide.region_4.6_spmd.clone, body=%wide.region_1.5_spmd.clone.sunk | while | flops 551571456 | bytes 19088480 | solution.py:141
  416.8 8.9 copy.126
  425.7 9.1 copy.102
  434.8 85.3 %while.113 = (s32[]{:T(128)}, f32[512,8,128]{0,2,1:T(8,128)}, bf16[8,512,8,128]{3,2,1,0:T(8,128)(2,1)}, bf16[8,512,8,128]{3,1,2,0:T(8,128)(2,1)}, bf16[512,8,128...) while((s32[]{:T(128)}, f32[512,8,128]{0,2,1:T(8,128)}, ...), condition=%wide.region_10.12_spmd.clone, body=%wide.region_9.11_spmd.clone.sunk | while | flops 1083179008 | bytes 11551851 | solution.py:141
  449.7 6.1 bitcast_add_fusion.12
  460.4 6.1 bitcast_add_fusion.12
  481.9 6.1 bitcast_add_fusion.12
  492.6 6.1 bitcast_add_fusion.12
  514.1 6.1 bitcast_add_fusion.12
  520.2 11.2 while.109
  525.1 6.3 bitcast_add_fusion.10
  545.4 11.5 multiply_convert_fusion
  569.2 48.3 %while.114 = (s32[]{:T(128)}, f32[8,512]{1,0:T(8,128)S(1)}, bf16[8,512,8,128]{3,1,2,0:T(8,128)(2,1)}, bf16[512,8,128]{2,0,1:T(8,128)(2,1)S(1)}, f32[8,512]{1,0:T...) while((s32[]{:T(128)}, f32[8,512]{1,0:T(8,128)S(1)}, ...), condition=%wide.region_17.19_spmd.clone, body=%wide.region_15.18_spmd.clone.sunk | while | flops 1084231680 | bytes 21055084 | solution.py:141
  618.5 13.1 while.110
  625.0 6.5 fusion.278
  631.6 106.0 %while.115 = (s32[]{:T(128)}, f32[512,8,128]{0,2,1:T(8,128)S(1)}, bf16[8,512,8,128]{3,1,2,0:T(8,128)(2,1)}, bf16[512,8,128]{2,0,1:T(8,128)(2,1)S(1)}, f32[8,512]...) while((s32[]{:T(128)}, f32[512,8,128]{0,2,1:T(8,128)S(1)}, ...), condition=%wide.region_22.24_spmd.clone, body=%wide.region_21.23_spmd.clone.sunk | while | flops 1624244224 | bytes 26249336 | solution.py:141
  637.3 7.5 bitcast_add_fusion.13
  650.6 7.5 bitcast_add_fusion.13
  663.8 7.5 bitcast_add_fusion.13
  677.1 7.5 bitcast_add_fusion.13
  690.3 7.5 bitcast_add_fusion.13
  703.6 7.5 bitcast_add_fusion.13
  716.8 7.5 bitcast_add_fusion.13
  730.1 7.5 bitcast_add_fusion.13
  743.4 22.3 %while.111 = (s32[]{:T(128)}, f32[512,8,128]{0,2,1:T(8,128)S(1)}, bf16[4,512,8,128]{3,1,2,0:T(8,128)(2,1)}, bf16[4,512,8,128]{3,1,2,0:T(8,128)(2,1)}, s32[]{:T(1...) while((s32[]{:T(128)}, f32[512,8,128]{0,2,1:T(8,128)S(1)}, ...), condition=%wide.region_24.26_spmd.clone, body=%wide.region_23.25_spmd.clone.sunk | while | flops 2706637824 | bytes 117236072 | solution.py:142
  749.6 6.7 fusion.290
  771.5 7.8 convolution_convert_fusion.1
  780.6 6.8 convolution_convert_fusion.2
  788.6 6.9 convolution_convert_fusion
  802.1 168.8 %reduce-scatter.22.cloned.1.call-done = bf16[1,512,8,128]{3,1,2,0:T(8,128)(2,1)} async-done(((bf16[4,512,8,128]{3,1,2,0:T(8,128)(2,1)}), bf16[1,512,8,128]{3,1,2,0:T(8,128)(2,1)}) %reduce-scatter.22.cloned.1.call-update) | async-done | bytes 1048592
  978.9 47.6 %reduce-scatter.24.cloned.1.call-done = bf16[1,512,8,128]{3,1,2,0:T(8,128)(2,1)} async-done(((bf16[4,512,8,128]{3,1,2,0:T(8,128)(2,1)}), bf16[1,512,8,128]{3,1,2,0:T(8,128)(2,1)}) %reduce-scatter.24.cloned.1.call-update) | async-done | bytes 1048592
  1039.4 25.3 %reduce-scatter.14.cloned.1.call-done = bf16[256,1024]{1,0:T(8,128)(2,1)} async-done(((bf16[1024,1024]{1,0:T(8,128)(2,1)}), bf16[256,1024]{1,0:T(8,128)(2,1)}) %reduce-scatter.14.cloned.1.call-update) | async-done | bytes 524304 | tf_op jit(solution)/shard_map/reduce_scatter | solution.py:266
  1064.7 68.5 %reduce-scatter.18.cloned.1.call-done = bf16[256,2816]{1,0:T(8,128)(2,1)} async-done(((bf16[1024,2816]{1,0:T(8,128)(2,1)}), bf16[256,2816]{1,0:T(8,128)(2,1)}) %reduce-scatter.18.cloned.1.call-update) | async-done | bytes 1441808 | tf_op jit(solution)/shard_map/reduce_scatter | solution.py:272
  1133.2 68.7 %reduce-scatter.16.cloned.1.call-done = bf16[256,2816]{1,0:T(8,128)(2,1)} async-done(((bf16[1024,2816]{1,0:T(8,128)(2,1)}), bf16[256,2816]{1,0:T(8,128)(2,1)}) %reduce-scatter.16.cloned.1.call-update) | async-done | bytes 1441808 | tf_op jit(solution)/shard_map/reduce_scatter | solution.py:269
  1201.9 68.5 %reduce-scatter.20.cloned.1.call-done = bf16[704,1024]{1,0:T(8,128)(2,1)} async-done(((bf16[2816,1024]{1,0:T(8,128)(2,1)}), bf16[704,1024]{1,0:T(8,128)(2,1)}) %reduce-scatter.20.cloned.1.call-update) | async-done | bytes 1441808 | tf_op jit(solution)/shard_map/reduce_scatter | solution.py:275
  1270.5 73.0 %reduce-scatter.12.cloned.1.call-done = bf16[256,3072]{1,0:T(8,128)(2,1)} async-done(((bf16[1024,3072]{1,0:T(8,128)(2,1)}), bf16[256,3072]{1,0:T(8,128)(2,1)}) %reduce-scatter.12.cloned.1.call-update) | async-done | bytes 1572880 | tf_op jit(solution)/shard_map/reduce_scatter | solution.py:263
  1345.5 7.8 fusion.166
  1353.3 8.1 fusion.157
  1361.4 8.9 all-reduce.6
  1370.4 15.4 %all-reduce.4 = (bf16[256]{0:T(256)(128)(2,1)S(1)}, bf16[256]{0:T(256)(128)(2,1)S(1)}) all-reduce(bf16[256]{0:T(256)(128)(2,1)S(1)} %dynamic-slice.5, bf16[256]{0:T(256)(128)(2,1)S(1)} %dynamic-slice.7), channel_id=1, replica_groups=mesh['seg'=8,'seq'=4] {'seg'}, use_global_device_ids=true, to_apply=%region_30.32 | all-reduce | flops 512 | bytes 2048 | tf_op jit(solution)/shard_map/psum | solution.py:280
  1390.5 94.6 %all-reduce.9.cloned.1.call-done = (bf16[256,3072]{1,0:T(8,128)(2,1)}, bf16[256,1024]{1,0:T(8,128)(2,1)}, bf16[256,2816]{1,0:T(8,128)(2,1)}, bf16[256,2816]{1,0:T(8,128)(2,1)}, bf16[704,1024]{1,0:T(8,128)(2,1)}) async-done(((bf16[256,3072]{1,0:T(8,128)(2,1)}, bf16[256,1024]{1,0:T(8,128)(2,1)}, bf16[256,2816]{1,0:T(8,128)(2,1)}, bf16[256,2816]{1,0:T(8,128)(2,1)}, bf16[704,1024]{1,0:T(8,128)(2,1)}), ...) | async-done | bytes 6422544 | tf_op jit(solution)/shard_map/psum | solution.py:282
  (336 shorter events, 417.6 us)
Async XLA Ops:
  7.2 526.1 %copy-start = (bf16[1024,1024]{1,0:T(8,128)(2,1)S(1)}, bf16[1024,1024]{1,0:T(8,128)(2,1)}, u32[]{:S(2)}) copy-start(bf16[1024,1024]{1,0:T(8,128)(2,1)} %param.36) | copy-start | bytes 6291460
  7.2 52.0 %all-gather.7.cloned.1.call-start = ((), (), s32[]{:S(2)}) async-start(), calls=%async_computation.7 | async-start | bytes 4718592 | tf_op jit(solution)/shard_map/all_gather | solution.py:85
  7.9 98.6 %all-gather.11.cloned.1.call-start = ((), (), s32[]{:S(2)}) async-start(), calls=%async_computation.9 | async-start | bytes 4718592 | tf_op jit(solution)/shard_map/all_gather | solution.py:84
  8.7 151.7 %all-gather.15.cloned.1.call-start = ((), (), s32[]{:S(2)}) async-start(), calls=%async_computation.11 | async-start | bytes 5242880 | tf_op jit(solution)/shard_map/all_gather | solution.py:106
  10.8 6.0 copy-start.43
  16.8 2.6 copy-start.11
  29.9 2.2 slice-start.2
  30.0 3.7 slice-start.3
  31.3 5.4 copy-start.7
  36.7 2.9 copy-start.46
  36.7 178.5 %all-gather.17.cloned.1.call-start = ((), (), s32[]{:S(2)}) async-start(), calls=%async_computation.12 | async-start | bytes 5242880 | tf_op jit(solution)/shard_map/all_gather | solution.py:107
  39.6 265.4 %all-gather.13.cloned.1.call-start = ((), (), s32[]{:S(2)}) async-start(), calls=%async_computation.10 | async-start | bytes 10485760 | tf_op jit(solution)/shard_map/all_gather | solution.py:90
  115.4 301.4 %all-gather.9.cloned.1.call-start = ((), (), s32[]{:S(2)}) async-start(), calls=%async_computation.8 | async-start | bytes 10485760 | tf_op jit(solution)/shard_map/all_gather | solution.py:91
  218.5 3.3 copy-start.3
  221.8 749.1 %reduce-scatter.22.cloned.1.call-start = ((), (), s32[]{:S(2)}) async-start(), calls=%async_computation.18 | async-start | bytes 5242880
  531.3 3.6 slice-start.4
  533.3 7.2 slice-start.6
  534.7 32.3 %copy-start.4 = (f32[512,1024]{1,0:T(8,128)}, f32[512,1024]{1,0:T(8,128)S(1)}, u32[]{:S(2)}) copy-start(f32[512,1024]{1,0:T(8,128)S(1)} %get-tuple-element.1348) | copy-start | bytes 6291460
  535.5 5.0 copy-start.32
  535.5 5.0 slice-start.7
  540.5 5.0 copy-start.28
  556.9 6.0 copy-start.50
  618.5 13.1 copy-start.2
  749.6 6.7 copy-start.9
  756.3 6.3 slice-start
  759.9 2.7 slice-start.1
  759.9 2.8 copy-start.35
  765.8 260.7 %reduce-scatter.24.cloned.1.call-start = ((), (), s32[]{:S(2)}) async-start(), calls=%async_computation.19 | async-start | bytes 5242880
  766.5 298.2 %reduce-scatter.14.cloned.1.call-start = ((), (), s32[]{:S(2)}) async-start(), calls=%async_computation.14 | async-start | bytes 2621440 | tf_op jit(solution)/shard_map/reduce_scatter | solution.py:266
  771.2 362.0 %reduce-scatter.18.cloned.1.call-start = ((), (), s32[]{:S(2)}) async-start(), calls=%async_computation.16 | async-start | bytes 7208960 | tf_op jit(solution)/shard_map/reduce_scatter | solution.py:272
  779.4 422.6 %reduce-scatter.16.cloned.1.call-start = ((), (), s32[]{:S(2)}) async-start(), calls=%async_computation.15 | async-start | bytes 7208960 | tf_op jit(solution)/shard_map/reduce_scatter | solution.py:269
  787.4 483.1 %reduce-scatter.20.cloned.1.call-start = ((), (), s32[]{:S(2)}) async-start(), calls=%async_computation.17 | async-start | bytes 7208960 | tf_op jit(solution)/shard_map/reduce_scatter | solution.py:275
  795.5 548.1 %reduce-scatter.12.cloned.1.call-start = ((), (), s32[]{:S(2)}) async-start(), calls=%async_computation.13 | async-start | bytes 7864320 | tf_op jit(solution)/shard_map/reduce_scatter | solution.py:263
  972.3 2.8 copy-start.18
  972.3 2.8 copy-start.26
  972.3 2.8 copy-start.27
  977.6 51.1 %copy-start.19 = (bf16[1,512,8,128]{3,1,2,0:T(8,128)(2,1)S(1)}, bf16[1,512,8,128]{3,1,2,0:T(8,128)(2,1)}, u32[]{:S(2)}) copy-start(bf16[1,512,8,128]{3,1,2,0:T(8,128)(2,1)} %reduce-scatter.22.cloned.1.call-done) | copy-start | bytes 3145732
  1028.4 2.6 copy-start.16
  1028.7 3.5 copy-start.38
  1039.1 446.0 %all-reduce.9.cloned.1.call-start = ((), (), s32[]{:S(2)}) async-start(), calls=%async_computation.20 | async-start | bytes 12845056 | tf_op jit(solution)/shard_map/psum | solution.py:282
  1345.4 7.8 copy-start.31
  1345.4 7.8 copy-start.37
  1345.5 7.8 copy-start.39
  1353.2 8.1 copy-start.47
  1353.3 33.7 %copy-start.15 = (f32[512,1024]{1,0:T(8,128)S(1)}, f32[512,1024]{1,0:T(8,128)}, u32[]{:S(2)}) copy-start(f32[512,1024]{1,0:T(8,128)} %copy-done.14) | copy-start | bytes 6291460
  1353.3 33.7 %copy-start.42 = (f32[512]{0:T(512)S(1)}, f32[512]{0:T(512)}, u32[]{:S(2)}) copy-start(f32[512]{0:T(512)} %get-tuple-element.1341) | copy-start | bytes 6148
  1485.1 3.6 copy-start.25
  1492.3 3.0 copy-start.1
  (25 other events, 42.2 us)
Sparse Core Ops, SparseCore 0:
  9.6 49.5 all-gather.6
  60.8 45.6 all-gather.10
  109.0 51.3 all-gather.14
  162.6 52.5 all-gather.16
  217.5 87.4 all-gather.12
  307.3 87.4 all-gather.8
  765.9 204.9 reduce-scatter.21
  973.8 52.5 reduce-scatter.23
  1029.5 35.1 reduce-scatter.13
  1067.5 65.6 reduce-scatter.17
  1136.2 65.6 reduce-scatter.15
  1204.8 65.6 reduce-scatter.19
  1273.5 70.0 reduce-scatter.11
  1346.1 138.8 all-reduce.8
where the time goes:
time: 1510 us; the launch traced here: 1500 us
  waiting for transfers between devices  854 us (57%)
  matrix products  377 us (25%)
  local copies, waits for them, and re-layouts  138 us (9%)
  other arithmetic  89.1 us (6%)
  blocking collectives  24.3 us (2%)
  between operations  16.4 us (1%)
    unnamed x16, waiting for transfers between devices  219 us
    dot_general x27, matrix products, block_scores(): jnp.einsum('qhd,khd->hqk', query_heads, key_block, preferred_element_type...  127 us
    psum x1, waiting for transfers between devices, on_device(): lax.psum(shares[2].astype(jnp.bfloat16), 'seg').astype(jnp.float32)  94.6 us
    all_gather x1, waiting for transfers between devices, on_device(): lax.all_gather(chosen_keys, 'seq', axis=1, tiled=True)  83.1 us
    reduce_scatter x1, waiting for transfers between devices, on_device(): lax.psum_scatter(grad_qkv.astype(jnp.bfloat16), 'seq', scatter_dimension=...  73 us
    unnamed x123, local copies, waits for them, and re-layouts  69.1 us
    reduce_scatter x1, waiting for transfers between devices, on_device(): lax.psum_scatter(grad_gate.astype(jnp.bfloat16), 'seq', scatter_dimension...  68.7 us
    reduce_scatter x1, waiting for transfers between devices, on_device(): lax.psum_scatter(grad_down.astype(jnp.bfloat16), 'seq', scatter_dimension...  68.5 us
  transfers between devices with their start and end apart: 14, of which 13 were waited for; matrix products, arithmetic and copies ran while one was open for 16% of the time, Pallas kernels for 0%

commit v1 on v0

--- a/solution.py
+++ b/solution.py
@@ -276,10 +276,15 @@
             grad_down.astype(jnp.bfloat16), "seq", scatter_dimension=0, tiled=True
         ).astype(jnp.float32),
     )
+
+    def track_sides_on_mesh(page, named_axis):
+        big = jnp.sum(lax.all_gather(page, axis_name=named_axis), axis=0)
+        return big
+
     totals = (
         lax.psum(shares[0].astype(jnp.bfloat16), "seg").astype(jnp.float32),
         lax.psum(shares[1].astype(jnp.bfloat16), "seg").astype(jnp.float32),
-        lax.psum(shares[2].astype(jnp.bfloat16), "seg").astype(jnp.float32),
+        track_sides_on_mesh(shares[2].astype(jnp.bfloat16), "seg").astype(jnp.float32),
         lax.psum(shares[3].astype(jnp.bfloat16), "seg").astype(jnp.float32),
         lax.psum(shares[4].astype(jnp.bfloat16), "seg").astype(jnp.float32),
         lax.psum(shares[5].astype(jnp.bfloat16), "seg").astype(jnp.float32),

time: 1510 us -> 1680 us (1.11)
  waiting for transfers between devices: 854 us -> 1010 us
    all_gather x0 -> x1, waiting for transfers between devices: none -> 109 us  [track_sides_on_mesh(): big = jnp.sum(lax.all_gather(page, axis_name=named_axis), axis=0)]
    all_gather x1, waiting for transfers between devices: 0.02 us -> 81.6 us  [on_device(): lax.all_gather(chosen_values, 'seq', axis=1, tiled=True)]
    psum x1, waiting for transfers between devices: 94.6 us -> 65.4 us  [on_device(): lax.psum(shares[3].astype(jnp.bfloat16), 'seg').astype(jnp.float32)]
    all_gather x1, waiting for transfers between devices: 43.1 us -> 18.8 us  [on_device(): lax.all_gather(mem_keys, 'seg', axis=0, tiled=True)]
    all_gather x1, waiting for transfers between devices: 19.3 us -> 43.1 us  [on_device(): lax.all_gather(mem_values, 'seg', axis=0, tiled=True)]
    unnamed x16 -> x17, waiting for transfers between devices: 219 us -> 224 us
    unnamed x123 -> x117, local copies, waits for them, and re-layouts: 69.1 us -> 69.9 us
  transfers between devices with their start and end apart: 14 -> 15, of which waited for: 13 -> 15; matrix products, arithmetic and copies ran while one was open for 16% -> 8% of each run, Pallas kernels for 0% -> 0%
where the time goes in v1:
time: 1680 us; the launch traced here: 1670 us
  waiting for transfers between devices  1010 us (60%)
  matrix products  376 us (22%)
  local copies, waits for them, and re-layouts  139 us (8%)
  other arithmetic  98.7 us (6%)
  blocking collectives  24.4 us (1%)
    unnamed x17, waiting for transfers between devices  224 us
    dot_general x27, matrix products, block_scores(): jnp.einsum('qhd,khd->hqk', query_heads, key_block, preferred_element_type...  127 us
    all_gather x1, waiting for transfers between devices, track_sides_on_mesh(): big = jnp.sum(lax.all_gather(page, axis_name=named_axis), axis=0)  109 us
    all_gather x1, waiting for transfers between devices, on_device(): lax.all_gather(chosen_values, 'seq', axis=1, tiled=True)  81.6 us
    all_gather x1, waiting for transfers between devices, on_device(): lax.all_gather(chosen_keys, 'seq', axis=1, tiled=True)  80.9 us
    reduce_scatter x1, waiting for transfers between devices, on_device(): lax.psum_scatter(grad_qkv.astype(jnp.bfloat16), 'seq', scatter_dimension=...  72.7 us
    unnamed x117, local copies, waits for them, and re-layouts  69.9 us
    reduce_scatter x1, waiting for transfers between devices, on_device(): lax.psum_scatter(grad_up.astype(jnp.bfloat16), 'seq', scatter_dimension=0...  68.7 us
  transfers between devices with their start and end apart: 15, of which 15 were waited for; matrix products, arithmetic and copies ran while one was open for 8% of the time, Pallas kernels for 0%

profile of v1, /device:TPU:0, one launch (start us, length us, event | category | flops | bytes accessed | tf_op | source)
XLA Modules:
  0.0 1672.4 jit_solution(14979190047099461669)
XLA Ops:
  40.4 18.8 %all-gather.13.cloned.1.call-done = bf16[8,256,1024]{2,1,0:T(8,128)(2,1)} async-done(((bf16[1,256,1024]{2,1,0:T(8,128)(2,1)}), bf16[8,256,1024]{2,1,0:T(8,128)(2,1)}) %all-gather.13.cloned.1.call-update) | async-done | bytes 4194320 | tf_op jit(solution)/shard_map/all_gather | solution.py:84
  63.4 43.1 %all-gather.9.cloned.1.call-done = bf16[8,256,1024]{2,1,0:T(8,128)(2,1)} async-done(((bf16[1,256,1024]{2,1,0:T(8,128)(2,1)}), bf16[8,256,1024]{2,1,0:T(8,128)(2,1)}) %all-gather.9.cloned.1.call-update) | async-done | bytes 4194320 | tf_op jit(solution)/shard_map/all_gather | solution.py:85
  119.2 41.2 %all-gather.17.cloned.1.call-done = bf16[2048,1024]{1,0:T(8,128)(2,1)} async-done(((bf16[512,1024]{1,0:T(8,128)(2,1)}), bf16[2048,1024]{1,0:T(8,128)(2,1)}) %all-gather.17.cloned.1.call-update) | async-done | bytes 4194320 | tf_op jit(solution)/shard_map/all_gather | solution.py:106
  166.5 48.7 %all-gather.19.cloned.1.call-done = bf16[2048,1024]{1,0:T(8,128)(2,1)} async-done(((bf16[512,1024]{1,0:T(8,128)(2,1)}), bf16[2048,1024]{1,0:T(8,128)(2,1)}) %all-gather.19.cloned.1.call-update) | async-done | bytes 4194320 | tf_op jit(solution)/shard_map/all_gather | solution.py:107
  223.4 81.6 %all-gather.11.cloned.1.call-done = bf16[4,1024,1024]{2,1,0:T(8,128)(2,1)} async-done(((bf16[4,256,1024]{2,1,0:T(8,128)(2,1)}), bf16[4,1024,1024]{2,1,0:T(8,128)(2,1)}) %all-gather.11.cloned.1.call-update) | async-done | bytes 8388624 | tf_op jit(solution)/shard_map/all_gather | solution.py:91
  305.0 8.9 copy.126
  313.9 80.9 %all-gather.15.cloned.1.call-done = bf16[4,1024,1024]{2,1,0:T(8,128)(2,1)} async-done(((bf16[4,256,1024]{2,1,0:T(8,128)(2,1)}), bf16[4,1024,1024]{2,1,0:T(8,128)(2,1)}) %all-gather.15.cloned.1.call-update) | async-done | bytes 8388624 | tf_op jit(solution)/shard_map/all_gather | solution.py:90
  394.8 8.9 copy.127
  403.7 9.0 copy.87
  412.7 87.6 %while.112 = (s32[]{:T(128)}, f32[8,512]{1,0:T(8,128)S(1)}, f32[8,512]{1,0:T(8,128)S(1)}, bf16[8,512,8,128]{3,1,2,0:T(8,128)(2,1)}, bf16[512,8,128]{2,0,1:T(8,128)(2,1)S(1)}, /*index=5*/pred[]{:T(512)}, s32[]{:T(128)}, s32[]{:T(128)}) while((s32[]{:T(128)}, f32[8,512]{1,0:T(8,128)S(1)}, f32[8,512]{1,0:T(8,128)S(1)}, ...), condition=%wide.region_4.6_spmd.clone, body=%wide.region_1.5_spmd.clone.sunk | while | flops 551571456 | bytes 19087980 | solution.py:141
  505.0 9.0 copy.102
  514.1 85.2 %while.113 = (s32[]{:T(128)}, f32[512,8,128]{0,2,1:T(8,128)}, bf16[8,512,8,128]{3,2,1,0:T(8,128)(2,1)}, bf16[8,512,8,128]{3,1,2,0:T(8,128)(2,1)}, bf16[512,8,128...) while((s32[]{:T(128)}, f32[512,8,128]{0,2,1:T(8,128)}, ...), condition=%wide.region_10.12_spmd.clone, body=%wide.region_9.11_spmd.clone.sunk | while | flops 1083179008 | bytes 11551351 | solution.py:141
  528.8 6.1 bitcast_add_fusion.12
  582.5 6.1 bitcast_add_fusion.12
  599.3 11.3 while.109
  604.3 6.3 bitcast_add_fusion.10
  624.8 11.9 multiply_convert_fusion
  648.1 48.3 %while.114 = (s32[]{:T(128)}, f32[8,512]{1,0:T(8,128)S(1)}, bf16[8,512,8,128]{3,1,2,0:T(8,128)(2,1)}, bf16[512,8,128]{2,0,1:T(8,128)(2,1)S(1)}, f32[8,512]{1,0:T...) while((s32[]{:T(128)}, f32[8,512]{1,0:T(8,128)S(1)}, ...), condition=%wide.region_17.19_spmd.clone, body=%wide.region_15.18_spmd.clone.sunk | while | flops 1084231680 | bytes 21054076 | solution.py:141
  697.3 13.1 while.110
  703.9 6.5 fusion.278
  710.4 106.0 %while.115 = (s32[]{:T(128)}, f32[512,8,128]{0,2,1:T(8,128)S(1)}, bf16[8,512,8,128]{3,1,2,0:T(8,128)(2,1)}, bf16[512,8,128]{2,0,1:T(8,128)(2,1)S(1)}, f32[8,512]...) while((s32[]{:T(128)}, f32[512,8,128]{0,2,1:T(8,128)S(1)}, ...), condition=%wide.region_22.24_spmd.clone, body=%wide.region_21.23_spmd.clone.sunk | while | flops 1624244224 | bytes 26249344 | solution.py:141
  716.2 7.5 bitcast_add_fusion.13
  729.4 7.5 bitcast_add_fusion.13
  742.6 7.5 bitcast_add_fusion.13
  755.9 7.5 bitcast_add_fusion.13
  769.1 7.5 bitcast_add_fusion.13
  782.4 7.5 bitcast_add_fusion.13
  795.6 7.5 bitcast_add_fusion.13
  808.9 7.5 bitcast_add_fusion.13
  822.2 22.7 %while.111 = (s32[]{:T(128)}, f32[512,8,128]{0,2,1:T(8,128)S(1)}, bf16[4,512,8,128]{3,1,2,0:T(8,128)(2,1)}, bf16[4,512,8,128]{3,1,2,0:T(8,128)(2,1)}, s32[]{:T(1...) while((s32[]{:T(128)}, f32[512,8,128]{0,2,1:T(8,128)S(1)}, ...), condition=%wide.region_24.26_spmd.clone, body=%wide.region_23.25_spmd.clone.sunk | while | flops 2706637824 | bytes 150790576 | solution.py:142
  828.4 6.7 fusion.290
  850.6 7.8 convolution_convert_fusion.2
  859.7 6.8 convolution_convert_fusion.1
  867.7 6.9 convolution_convert_fusion
  881.2 169.2 %reduce-scatter.24.cloned.1.call-done = bf16[1,512,8,128]{3,1,2,0:T(8,128)(2,1)} async-done(((bf16[4,512,8,128]{3,1,2,0:T(8,128)(2,1)}), bf16[1,512,8,128]{3,1,2,0:T(8,128)(2,1)}) %reduce-scatter.24.cloned.1.call-update) | async-done | bytes 1048592
  1053.6 52.4 %reduce-scatter.22.cloned.1.call-done = bf16[1,512,8,128]{3,1,2,0:T(8,128)(2,1)} async-done(((bf16[4,512,8,128]{3,1,2,0:T(8,128)(2,1)}), bf16[1,512,8,128]{3,1,2,0:T(8,128)(2,1)}) %reduce-scatter.22.cloned.1.call-update) | async-done | bytes 1048592
  1121.6 22.7 %reduce-scatter.14.cloned.1.call-done = bf16[256,1024]{1,0:T(8,128)(2,1)} async-done(((bf16[1024,1024]{1,0:T(8,128)(2,1)}), bf16[256,1024]{1,0:T(8,128)(2,1)}) %reduce-scatter.14.cloned.1.call-update) | async-done | bytes 524304 | tf_op jit(solution)/shard_map/reduce_scatter | solution.py:266
  1144.2 68.5 %reduce-scatter.16.cloned.1.call-done = bf16[256,2816]{1,0:T(8,128)(2,1)} async-done(((bf16[1024,2816]{1,0:T(8,128)(2,1)}), bf16[256,2816]{1,0:T(8,128)(2,1)}) %reduce-scatter.16.cloned.1.call-update) | async-done | bytes 1441808 | tf_op jit(solution)/shard_map/reduce_scatter | solution.py:269
  1212.8 68.7 %reduce-scatter.18.cloned.1.call-done = bf16[256,2816]{1,0:T(8,128)(2,1)} async-done(((bf16[1024,2816]{1,0:T(8,128)(2,1)}), bf16[256,2816]{1,0:T(8,128)(2,1)}) %reduce-scatter.18.cloned.1.call-update) | async-done | bytes 1441808 | tf_op jit(solution)/shard_map/reduce_scatter | solution.py:272
  1281.5 68.5 %reduce-scatter.20.cloned.1.call-done = bf16[704,1024]{1,0:T(8,128)(2,1)} async-done(((bf16[2816,1024]{1,0:T(8,128)(2,1)}), bf16[704,1024]{1,0:T(8,128)(2,1)}) %reduce-scatter.20.cloned.1.call-update) | async-done | bytes 1441808 | tf_op jit(solution)/shard_map/reduce_scatter | solution.py:275
  1350.4 72.7 %reduce-scatter.12.cloned.1.call-done = bf16[256,3072]{1,0:T(8,128)(2,1)} async-done(((bf16[1024,3072]{1,0:T(8,128)(2,1)}), bf16[256,3072]{1,0:T(8,128)(2,1)}) %reduce-scatter.12.cloned.1.call-update) | async-done | bytes 1572880 | tf_op jit(solution)/shard_map/reduce_scatter | solution.py:263
  1424.4 7.8 fusion.166
  1432.2 8.1 fusion.157
  1440.3 8.9 all-reduce.6
  1449.4 15.4 all-reduce.4
  1469.4 65.4 %all-reduce.9.cloned.1.call-done = (bf16[256,1024]{1,0:T(8,128)(2,1)}, bf16[256,2816]{1,0:T(8,128)(2,1)}, bf16[256,2816]{1,0:T(8,128)(2,1)}, bf16[704,1024]{1,0:T(8,128)(2,1)}) async-done(((bf16[256,1024]{1,0:T(8,128)(2,1)}, bf16[256,2816]{1,0:T(8,128)(2,1)}, bf16[256,2816]{1,0:T(8,128)(2,1)}, bf16[704,1024]{1,0:T(8,128)(2,1)}), (bf16[256,1024]{1,0:T(8,128)(2,1)}, bf16[256,2816]{1,0:T(8,128)(2,1)}, ...) | async-done | bytes 4849680 | tf_op jit(solution)/shard_map/psum | solution.py:288
  1544.0 109.1 %all-gather.21.cloned.1.call-done = bf16[2048,3072]{1,0:T(8,128)(2,1)} async-done(((bf16[256,3072]{1,0:T(8,128)(2,1)}), bf16[2048,3072]{1,0:T(8,128)(2,1)}) %all-gather.21.cloned.1.call-update) | async-done | bytes 12582928 | tf_op jit(solution)/shard_map/all_gather | solution.py:281
  1653.1 8.9 reduce_sum.116
  (338 shorter events, 437.3 us)
Async XLA Ops:
  7.2 605.3 %copy-start = (bf16[1024,1024]{1,0:T(8,128)(2,1)S(1)}, bf16[1024,1024]{1,0:T(8,128)(2,1)}, u32[]{:S(2)}) copy-start(bf16[1024,1024]{1,0:T(8,128)(2,1)} %param.36) | copy-start | bytes 6291460
  7.2 52.0 %all-gather.13.cloned.1.call-start = ((), (), s32[]{:S(2)}) async-start(), calls=%async_computation.9 | async-start | bytes 4718592 | tf_op jit(solution)/shard_map/all_gather | solution.py:84
  7.9 98.6 %all-gather.9.cloned.1.call-start = ((), (), s32[]{:S(2)}) async-start(), calls=%async_computation.7 | async-start | bytes 4718592 | tf_op jit(solution)/shard_map/all_gather | solution.py:85
  8.7 151.7 %all-gather.17.cloned.1.call-start = ((), (), s32[]{:S(2)}) async-start(), calls=%async_computation.11 | async-start | bytes 5242880 | tf_op jit(solution)/shard_map/all_gather | solution.py:106
  17.4 2.6 copy-start.13
  30.5 3.7 slice-start.3
  31.8 5.4 copy-start.7
  37.3 2.9 copy-start.45
  37.3 178.0 %all-gather.19.cloned.1.call-start = ((), (), s32[]{:S(2)}) async-start(), calls=%async_computation.12 | async-start | bytes 5242880 | tf_op jit(solution)/shard_map/all_gather | solution.py:107
  40.1 264.9 %all-gather.11.cloned.1.call-start = ((), (), s32[]{:S(2)}) async-start(), calls=%async_computation.8 | async-start | bytes 10485760 | tf_op jit(solution)/shard_map/all_gather | solution.py:91
  115.4 279.4 %all-gather.15.cloned.1.call-start = ((), (), s32[]{:S(2)}) async-start(), calls=%async_computation.10 | async-start | bytes 10485760 | tf_op jit(solution)/shard_map/all_gather | solution.py:90
  116.0 934.4 %reduce-scatter.24.cloned.1.call-start = ((), (), s32[]{:S(2)}) async-start(), calls=%async_computation.20 | async-start | bytes 5242880
  610.6 3.6 slice-start.4
  612.5 7.2 slice-start.6
  613.9 32.0 %copy-start.4 = (f32[512,1024]{1,0:T(8,128)}, f32[512,1024]{1,0:T(8,128)S(1)}, u32[]{:S(2)}) copy-start(f32[512,1024]{1,0:T(8,128)S(1)} %get-tuple-element.1347) | copy-start | bytes 6291460
  614.7 5.0 copy-start.32
  614.7 5.0 slice-start.7
  619.8 5.0 copy-start.28
  636.7 5.1 copy-start.49
  697.3 13.1 copy-start.2
  828.4 11.1 slice-start
  835.1 2.7 copy-start.9
  835.1 4.4 slice-start.1
  837.8 2.5 copy-start.11
  837.8 2.7 copy-start.35
  839.4 3.4 copy-start.10
  844.9 261.1 %reduce-scatter.22.cloned.1.call-start = ((), (), s32[]{:S(2)}) async-start(), calls=%async_computation.19 | async-start | bytes 5242880
  845.7 298.6 %reduce-scatter.14.cloned.1.call-start = ((), (), s32[]{:S(2)}) async-start(), calls=%async_computation.14 | async-start | bytes 2621440 | tf_op jit(solution)/shard_map/reduce_scatter | solution.py:266
  850.4 362.4 %reduce-scatter.16.cloned.1.call-start = ((), (), s32[]{:S(2)}) async-start(), calls=%async_computation.15 | async-start | bytes 7208960 | tf_op jit(solution)/shard_map/reduce_scatter | solution.py:269
  858.5 422.9 %reduce-scatter.18.cloned.1.call-start = ((), (), s32[]{:S(2)}) async-start(), calls=%async_computation.16 | async-start | bytes 7208960 | tf_op jit(solution)/shard_map/reduce_scatter | solution.py:272
  866.5 483.5 %reduce-scatter.20.cloned.1.call-start = ((), (), s32[]{:S(2)}) async-start(), calls=%async_computation.17 | async-start | bytes 7208960 | tf_op jit(solution)/shard_map/reduce_scatter | solution.py:275
  874.6 548.4 %reduce-scatter.12.cloned.1.call-start = ((), (), s32[]{:S(2)}) async-start(), calls=%async_computation.13 | async-start | bytes 7864320 | tf_op jit(solution)/shard_map/reduce_scatter | solution.py:263
  1107.4 2.8 copy-start.19
  1107.4 2.8 copy-start.26
  1107.4 2.8 copy-start.27
  1111.8 2.9 copy-start.38
  1121.5 413.3 %all-reduce.9.cloned.1.call-start = ((), (), s32[]{:S(2)}) async-start(), calls=%async_computation.21 | async-start | bytes 9699328 | tf_op jit(solution)/shard_map/psum | solution.py:288
  1350.0 73.1 %copy-start.48 = (u32[32]{0:T(128)S(1)}, u32[32]{0:T(128)}, u32[]{:S(2)}) copy-start(u32[32]{0:T(128)} %constant.287) | copy-start | bytes 388
  1350.0 74.3 %copy-start.5 = (f32[512,1024]{1,0:T(8,128)S(1)}, f32[512,1024]{1,0:T(8,128)}, u32[]{:S(2)}) copy-start(f32[512,1024]{1,0:T(8,128)} %copy-done.4) | copy-start | bytes 6291460
  1350.0 303.1 %all-gather.21.cloned.1.call-start = ((), (), s32[]{:S(2)}) async-start(), calls=%async_computation.18 | async-start | bytes 14155776 | tf_op jit(solution)/shard_map/all_gather | solution.py:281
  1424.3 7.8 copy-start.31
  1424.4 7.8 copy-start.37
  1424.4 7.8 copy-start.39
  1432.2 8.1 copy-start.46
  1432.2 33.8 %copy-start.17 = (f32[512,1024]{1,0:T(8,128)S(1)}, f32[512,1024]{1,0:T(8,128)}, u32[]{:S(2)}) copy-start(f32[512,1024]{1,0:T(8,128)} %copy-done.16) | copy-start | bytes 6291460
  1432.2 33.8 %copy-start.41 = (f32[512]{0:T(512)S(1)}, f32[512]{0:T(512)}, u32[]{:S(2)}) copy-start(f32[512]{0:T(512)} %get-tuple-element.1340) | copy-start | bytes 6148
  1534.8 5.4 copy-start.25
  1653.1 12.3 copy-start.1
  (25 other events, 42.7 us)
Sparse Core Ops, SparseCore 0:
  9.6 49.5 all-gather.12
  60.8 45.6 all-gather.8
  109.0 51.3 all-gather.16
  162.6 52.5 all-gather.18
  217.5 87.4 all-gather.10
  307.3 87.4 all-gather.14
  845.0 205.3 reduce-scatter.23
  1053.4 52.5 reduce-scatter.21
  1109.0 35.1 reduce-scatter.13
  1147.0 65.6 reduce-scatter.15
  1215.7 65.6 reduce-scatter.17
  1284.3 65.6 reduce-scatter.19
  1353.0 70.0 reduce-scatter.11
  1425.6 109.1 all-reduce.8
  1536.3 116.7 all-gather.20
